TPU v7x, 128 devices: a whole 4x4x4 slice. The times are simulated.
128 devices in a mesh: kv: 2 (over y_lo), ctx: 64 (over z, x, y_hi, core).
Axes of the slice: x: 4, y: 4 (y_hi: 2, y_lo: 2; y = y_hi * 2 + y_lo), z: 4, core: 2. Of those that a mesh axis runs over, the one named last changes fastest.
Arguments:
- residual: bfloat16 [64, 8192], P(None, 'ctx'), may hold values from -8 to 8
- queries: bfloat16 [64, 8192], P(None, 'kv'), may hold values from -16 to 16
- draft_token_keys: bfloat16 [64, 1024], P(None, 'kv'), may hold values from -32 to 32
- draft_token_values: bfloat16 [64, 1024], P(None, 'kv'), may hold values from -8 to 8
- cache_keys: bfloat16 [2, 32768, 1024], P(None, 'ctx', 'kv'), may hold values from -32 to 32
- cached_value_rows: bfloat16 [2, 32768, 1024], P(None, 'ctx', 'kv'), may hold values from -8 to 8
- tenant_ids: int32 [64], replicated, may hold values from 0 to 1, as said below
- tree_mask: int32 [64, 64], replicated, may hold values from 0 to 1, as said below
- cache_lengths: int32 [2], replicated, may hold values from 16385 to 32768
- out_weight: bfloat16 [8192, 8192], P('kv', 'ctx'), may hold values from -0.0625 to 0.0625
- out_signs: bfloat16 [2, 8192, 8192], P(None, 'kv', 'ctx'), may hold values from -1 to 1, as said below
- norm_gain: float32 [8192], P('ctx'), may hold values from 0.1 to 1.9
- gate_weight: bfloat16 [8192, 16384], P(None, ('kv', 'ctx')), may hold values from -0.0625 to 0.0625
- up_weight: bfloat16 [8192, 16384], P(None, ('kv', 'ctx')), may hold values from -0.0625 to 0.0625
- down_weight: bfloat16 [16384, 8192], P(('kv', 'ctx')), may hold values from -0.1875 to 0.1875
- gate_signs: bfloat16 [2, 8192, 16384], P(None, None, ('kv', 'ctx')), may hold values from -1 to 1, as said below
- up_signs: bfloat16 [2, 8192, 16384], P(None, None, ('kv', 'ctx')), may hold values from -1 to 1, as said below
- down_signs: bfloat16 [2, 16384, 8192], P(None, ('kv', 'ctx')), may hold values from -1 to 1, as said below
- delta_scale: float32 [2, 4], replicated, may hold values from 0.3 to 0.9
Outputs:
- mixed: bfloat16 [64, 8192], P(None, 'ctx')
Inputs may be any that keep to these rules, and one draw needn't show every extreme that they name: `tenant_ids`: exactly 32 tokens belong to each tenant. `tree_mask`: entry (i, j) is 1 exactly when token j is token i or an ancestor of token i in the draft tree of their common tenant; each tenant's 32 tokens form one tree. `out_signs`: every entry is 1 or -1. `gate_signs`: every entry is 1 or -1. `up_signs`: every entry is 1 or -1. `down_signs`: every entry is 1 or -1.
All inputs are finite; a program needn't handle non-finite values.
Results may differ from a plain program's by a relative error of at most 0.013.
Values may be sent and summed in bfloat16 or wider, within the bound.
A program may use at most 128 MiB of HBM per device.

v0:
```python
import jax
import jax.numpy as jnp
from jax import lax
from jax.sharding import PartitionSpec as P

D = 8192
QUERY_HEADS = 64
HEAD_SIZE = 128
FF = 16384
NEG = -1e30
EPS = 1e-05


def sent_together(arrays, axis, split_dim, concat_dim, along):
    columns = [a.reshape(*a.shape[:along], -1) for a in arrays]
    both = jnp.concatenate(columns, axis=along)
    filled, at, done = (
        lax.all_to_all(both, axis, split_axis=split_dim, concat_axis=concat_dim, tiled=True),
        0,
        [],
    )
    for a, column in zip(arrays, columns):
        share = filled[..., at : at + column.shape[along]]
        done.append(share.reshape(*share.shape[:along], *a.shape[along:]))
        at += column.shape[along]
    return tuple(done)


def sent_to_all(shard, axis):
    copies = jnp.broadcast_to(shard, (lax.axis_size(axis), *shard.shape))
    return lax.all_to_all(copies, axis, split_axis=0, concat_axis=0, tiled=True)


def laid_out(tiles, dim):
    tiles = jnp.moveaxis(tiles, 0, dim)
    shape = tiles.shape
    return tiles.reshape(*shape[:dim], shape[dim] * shape[dim + 1], *shape[dim + 2 :])


def collect(shard, axis, dim):
    tiles = sent_to_all(shard, axis)
    return laid_out(tiles, dim)


def of_everyone(shard, axis):
    return sent_to_all(shard, axis).astype(jnp.float32).sum(axis=0)


def of_everyone_2(shard, axis):
    everything = sent_to_all(shard, axis)
    return jnp.sum(everything, axis=0)


def cut_along(shard, dim, peers):
    before, after = (shard.shape[:dim], shard.shape[dim + 1 :])
    return jnp.moveaxis(shard.reshape(*before, peers, -1, *after), dim, 0)


def sum_at_owner(shard, axis, dim):
    tiles = cut_along(shard, dim, lax.axis_size(axis))
    arrived = lax.all_to_all(tiles, axis, split_axis=0, concat_axis=0, tiled=True)
    return arrived.sum(axis=0)


def combine(first, second):
    first_top, first_total, first_out = first
    second_top, second_total, second_out = second
    peak = jnp.maximum(first_top, second_top)
    first_scale = jnp.exp(first_top - peak)
    second_scale = jnp.exp(second_top - peak)
    total = first_total * first_scale + second_total * second_scale
    merged = first_out * first_scale[..., None] + second_out * second_scale[..., None]
    return (peak, total, merged)


def draft_rows(query_rows, group_rows, visible_rows, key_rows, value_rows, factor):
    groups = key_rows.shape[1]
    choose = (group_rows[:, None] == jnp.arange(groups, dtype=jnp.int32)[None, :]).astype(
        jnp.float32
    )
    every_group = (
        jnp.einsum("rd,kgd->rgk", query_rows, key_rows, preferred_element_type=jnp.float32) * factor
    )
    scores = jnp.einsum("rgk,rg->rk", every_group, choose, precision=lax.Precision.HIGHEST)
    masked = jnp.where(visible_rows, scores, NEG)
    peak = jnp.max(masked, axis=-1)
    weights = jnp.where(visible_rows, jnp.exp(masked - peak[:, None]), 0.0)
    total = jnp.sum(weights, axis=-1)
    every_value = jnp.einsum(
        "rk,kgd->rgd", weights.astype(jnp.bfloat16), value_rows, preferred_element_type=jnp.float32
    )
    result = jnp.einsum("rgd,rg->rd", every_value, choose, precision=lax.Precision.HIGHEST)
    return (peak, total, result)


def shards(
    residual,
    queries,
    draft_token_keys,
    draft_token_values,
    cache_keys,
    cached_value_rows,
    tenant_ids,
    tree_mask,
    cache_lengths,
    out_weight,
    out_signs,
    norm_gain,
    gate_weight,
    up_weight,
    down_weight,
    gate_signs,
    up_signs,
    down_signs,
    delta_scale,
):
    tenants = cache_keys.shape[0]
    tokens = tenant_ids.shape[0]
    draft = tokens // tenants
    heads_here = queries.shape[1] // HEAD_SIZE
    groups_here = draft_token_keys.shape[1] // HEAD_SIZE
    group_width = heads_here // groups_here
    ctx_rows = cache_keys.shape[1]
    factor = HEAD_SIZE ** (-0.5)
    sort_order = jnp.argsort(tenant_ids, stable=True)
    inverse = jnp.argsort(sort_order)
    sorted_queries = queries[sort_order]
    query_blocks = sorted_queries.reshape(tenants, draft, groups_here, group_width, HEAD_SIZE)
    draft_key_lines = draft_token_keys[sort_order].reshape(tokens, groups_here, HEAD_SIZE)
    draft_value_lines = draft_token_values[sort_order].reshape(tokens, groups_here, HEAD_SIZE)
    visible = tree_mask[sort_order][:, sort_order] > 0
    first_slot = lax.axis_index("ctx") * ctx_rows
    slot_ids = first_slot + jnp.arange(ctx_rows, dtype=jnp.int32)
    live = (slot_ids[None, :] < cache_lengths[:, None])[:, None, None, None, :]
    cache_key_blocks = cache_keys.reshape(tenants, ctx_rows, groups_here, HEAD_SIZE)
    cache_value_blocks = cached_value_rows.reshape(tenants, ctx_rows, groups_here, HEAD_SIZE)
    scores = (
        jnp.einsum(
            "tqgwd,tjgd->tqgwj", query_blocks, cache_key_blocks, preferred_element_type=jnp.float32
        )
        * factor
    )
    masked = jnp.where(live, scores, NEG)
    peak = jnp.max(masked, axis=-1)
    weights = jnp.where(live, jnp.exp(masked - peak[..., None]), 0.0)
    total = jnp.sum(weights, axis=-1)
    weighted = jnp.einsum(
        "tqgwj,tjgd->tqgwd",
        weights.astype(jnp.bfloat16),
        cache_value_blocks,
        preferred_element_type=jnp.float32,
    )
    part_top = peak.reshape(tokens, heads_here)
    part_total = total.reshape(tokens, heads_here)
    part_out = weighted.reshape(tokens, heads_here, HEAD_SIZE)
    n_ctx = lax.axis_size("ctx")
    all_rows = tokens * heads_here
    share = all_rows // n_ctx
    got_top, got_total, got_out = (
        lax.all_to_all(
            part_top.reshape(1, all_rows), "ctx", split_axis=1, concat_axis=0, tiled=True
        ),
        *sent_together(
            (part_total.reshape(1, all_rows), part_out.reshape(1, all_rows, HEAD_SIZE)),
            "ctx",
            1,
            0,
            2,
        ),
    )
    summit = jnp.max(got_top, axis=0)
    rescale = jnp.exp(got_top - summit)
    merged = (
        summit,
        jnp.sum(got_total * rescale, axis=0),
        jnp.sum(got_out * rescale[..., None], axis=0),
    )
    first_row = lax.axis_index("ctx") * share
    row_ids = first_row + jnp.arange(share, dtype=jnp.int32)
    token_rows = row_ids // heads_here
    group_rows = row_ids % heads_here // group_width
    query_rows = lax.dynamic_slice_in_dim(
        sorted_queries.reshape(all_rows, HEAD_SIZE), first_row, share, 0
    )
    own = draft_rows(
        query_rows, group_rows, visible[token_rows], draft_key_lines, draft_value_lines, factor
    )
    final_top, final_total, final_out = combine(merged, own)
    finished = (final_out / final_total[:, None]).astype(jnp.bfloat16)
    attention = collect(finished, "ctx", 0).reshape(tokens, heads_here * HEAD_SIZE)
    attention_split = attention.reshape(tenants, draft, -1)
    projected = jnp.dot(attention, out_weight, preferred_element_type=jnp.float32)
    out_delta = jnp.einsum(
        "tqh,thf->tqf", attention_split, out_signs, preferred_element_type=jnp.float32
    )
    projected = projected + (
        out_delta * (delta_scale[:, 0] * (QUERY_HEADS * HEAD_SIZE) ** (-0.5))[:, None, None]
    ).reshape(tokens, -1)
    summed_heads = of_everyone(projected.astype(jnp.bfloat16), "kv").astype(jnp.float32)
    hidden = residual[sort_order].astype(jnp.float32) + summed_heads
    squares = of_everyone_2(jnp.sum(hidden * hidden, axis=1), "ctx")
    normed = (hidden * lax.rsqrt(squares / D + EPS)[:, None] * norm_gain).astype(jnp.bfloat16)
    hidden_units = gate_weight.shape[1]
    piece = lax.all_gather(normed, "ctx", axis=1, tiled=True)
    size = piece.shape[1]
    split_piece = piece.reshape(tenants, draft, size)
    gate_base = jnp.dot(piece, gate_weight, preferred_element_type=jnp.float32)
    up_base = jnp.dot(piece, up_weight, preferred_element_type=jnp.float32)
    gate_delta = jnp.einsum(
        "tqf,tfh->tqh", split_piece, gate_signs, preferred_element_type=jnp.float32
    )
    up_delta = jnp.einsum("tqf,tfh->tqh", split_piece, up_signs, preferred_element_type=jnp.float32)
    gate = gate_base + (gate_delta * (delta_scale[:, 1] * D ** (-0.5))[:, None, None]).reshape(
        tokens, hidden_units
    )
    up_part = up_base + (up_delta * (delta_scale[:, 2] * D ** (-0.5))[:, None, None]).reshape(
        tokens, hidden_units
    )
    active = (jax.nn.silu(gate) * up_part).astype(jnp.bfloat16)
    active_split = active.reshape(tenants, draft, hidden_units)
    down_factor = delta_scale[:, 3] * FF ** (-0.5)
    features_here = residual.shape[1]
    base_part = lax.dot_general(
        down_weight, active, (((0,), (1,)), ((), ())), preferred_element_type=jnp.float32
    )
    delta_part = jnp.einsum(
        "thf,tqh->ftq", down_signs, active_split, preferred_element_type=jnp.float32
    )
    delta_part = delta_part * down_factor[None, :, None]
    lowered = sum_at_owner(
        base_part + delta_part.reshape(features_here * lax.axis_size("ctx"), tokens), "ctx", 0
    )
    lowered = of_everyone(lowered.astype(jnp.bfloat16), "kv").astype(jnp.float32)
    return (hidden + lowered.T).astype(jnp.bfloat16)[inverse]


def solution(mesh):
    return jax.shard_map(
        shards,
        mesh=mesh,
        in_specs=(
            P(None, "ctx"),
            P(None, "kv"),
            P(None, "kv"),
            P(None, "kv"),
            P(None, "ctx", "kv"),
            P(None, "ctx", "kv"),
            P(),
            P(),
            P(),
            P("kv", "ctx"),
            P(None, "kv", "ctx"),
            P("ctx"),
            P(None, ("kv", "ctx")),
            P(None, ("kv", "ctx")),
            P(("kv", "ctx"), None),
            P(None, None, ("kv", "ctx")),
            P(None, None, ("kv", "ctx")),
            P(None, ("kv", "ctx"), None),
            P(),
        ),
        out_specs=P(None, "ctx"),
        check_vma=False,
    )
```

profile of v0, /device:TPU:0, one launch (start us, length us, event | category | flops | bytes accessed | tf_op | source)
XLA Modules:
  0.0 268.2 jit_solution(5693490985125798498)
XLA Ops:
  6.5 2.8 %sort.34 = (s32[64]{0:T(128)}, s32[64]{0:T(128)S(1)}) sort(s32[64]{0:T(128)} %param.25, s32[64]{0:T(128)S(1)} %iota.25), dimensions={0}, to_apply=%region_0.0 | sort | flops 384 | bytes 1024 | tf_op jit(solution)/shard_map/jit(argsort)/sort | solution.py:125
  9.4 2.2 reshape.251
  11.6 0.9 gather_fusion.1
  12.6 4.0 %bitcast_reduce_fusion = (f32[2,32,4,8]{3,1,2,0:T(8,128)S(1)}, f32[2,4,32,8,512]{4,3,2,1,0:T(8,128)}) fusion(pred[2,512]{1,0:T(4,128)(4,1)S(1)} %broadcast_compare_fusion, bf16[2,512,4,128,1]{3,2,1,0,4:T(4,128)(2,1)} %bitcast.117, bf16[2,32,4,8,128]{4,3,2,1,0:T(8,128)(2,1)S(1)} %bitcast.119), kind=kOutput, calls=%fused_computation.12 | convolution fusion | flops 271579136 | bytes 5776384 | tf_op jit(solution)/shard_map/tqgwd,tjgd->tqgwj/dot_general | solution.py:138
  16.8 0.7 copy.96
  17.5 11.5 %all-to-all-start.1 = ((f32[1,64,32]{2,0,1:T(1,128)}), f32[1,64,32]{2,0,1:T(1,128)S(1)}, u32[]{:S(2)}, u32[]{:S(2)}) async-start(f32[1,64,32]{2,0,1:T(1,128)} %copy.96), calls=%async_computation.1 | async-start | bytes 65536 | tf_op jit(solution)/shard_map/all_to_all | solution.py:160
  29.0 1.0 reshape.254
  30.7 0.6 gather_fusion.3
  31.4 0.7 gather_fusion.5
  32.1 1.3 reshape.252
  33.5 3.5 %fusion.4 = f32[2,32,4,8]{3,1,2,0:T(8,128)S(1)} fusion(f32[2,4,32,8,512]{4,3,2,1,0:T(8,128)} %get-tuple-element.19, f32[2,32,4,8]{3,1,2,0:T(8,128)S(1)} %get-tuple-element.18, pred[2,512]{1,0:T(4,128)(4,1)S(1)} %broadcast_compare_fusion), kind=kLoop, calls=%fused_computation.17 | loop fusion | flops 5240832 | bytes 4211712 | tf_op jit(solution)/shard_map/reduce_sum | solution.py:146
  37.0 1.3 fusion.10
  38.5 1.3 reshape_reshape_reshape.8
  39.9 3.2 %pad_maximum_fusion = f32[1,2048,129]{2,1,0:T(8,128)} fusion(f32[1,2048,128]{2,1,0:T(8,128)S(1)} %bitcast.118, f32[1,2048,1]{2,1,0:T(8,128)} %reshape_reshape_reshape.8), kind=kLoop, calls=%fused_computation.19 | loop fusion | flops 264192 | bytes 2113536 | tf_op jit(solution)/shard_map/concatenate | solution.py:16
  43.1 0.8 fusion.13
  44.1 0.7 gather_fusion.6
  44.8 4.8 %copy.94 = f32[1,2048,129]{2,0,1:T(1,128)} copy(f32[1,2048,129]{2,1,0:T(8,128)} %pad_maximum_fusion) | data formatting | bytes 2113536 | tf_op jit(solution)/shard_map/concatenate | solution.py:16
  50.2 10.6 %all-to-all-start = ((f32[1,2048,129]{2,0,1:T(1,128)}), f32[1,2048,129]{2,0,1:T(1,128)}, u32[]{:S(2)}, u32[]{:S(2)}) async-start(f32[1,2048,129]{2,0,1:T(1,128)} %copy.94), calls=%async_computation | async-start | bytes 4194304 | tf_op jit(solution)/shard_map/all_to_all | solution.py:18
  62.1 28.9 %all-to-all-done = f32[1,2048,129]{2,0,1:T(1,128)} async-done(((f32[1,2048,129]{2,0,1:T(1,128)}), f32[1,2048,129]{2,0,1:T(1,128)}, u32[]{:S(2)}, u32[]{:S(2)}) %all-to-all-start) | async-done | bytes 1056800 | tf_op jit(solution)/shard_map/all_to_all | solution.py:18
  90.9 1.7 copy.118
  92.7 1.3 copy-done.4
  94.1 0.6 copy.103
  95.0 2.2 fusion.17
  97.3 0.9 broadcast_in_dim.76
  98.2 5.5 %all-to-all-start.2 = ((bf16[64,32,128]{2,1,0:T(8,128)(2,1)}), bf16[64,32,128]{2,1,0:T(8,128)(2,1)S(1)}, u32[]{:S(2)}, u32[]{:S(2)}) async-start(bf16[64,32,128]{2,1,0:T(8,128)(2,1)} %broadcast_in_dim.76), calls=%async_computation.2 | async-start | bytes 1048576 | tf_op jit(solution)/shard_map/all_to_all | solution.py:31
  104.0 13.7 %all-to-all-done.2 = bf16[64,32,128]{2,1,0:T(8,128)(2,1)S(1)} async-done(((bf16[64,32,128]{2,1,0:T(8,128)(2,1)}), bf16[64,32,128]{2,1,0:T(8,128)(2,1)S(1)}, u32[]{:S(2)}, u32[]{:S(2)}) %all-to-all-start.2) | async-done | bytes 524320 | tf_op jit(solution)/shard_map/all_to_all | solution.py:31
  117.9 2.0 convolution_multiply_fusion.4
  120.0 1.6 fusion.16
  122.2 3.3 %all-to-all-start.3 = ((bf16[2,64,128]{2,1,0:T(8,128)(2,1)}), bf16[2,64,128]{2,1,0:T(8,128)(2,1)S(1)}, u32[]{:S(2)}, u32[]{:S(2)}) async-start(bf16[2,64,128]{2,1,0:T(8,128)(2,1)} %broadcast_in_dim.77), calls=%async_computation.3 | async-start | bytes 65536 | tf_op jit(solution)/shard_map/all_to_all | solution.py:31
  125.5 0.6 gather_fusion
  126.1 3.2 %all-to-all-done.3 = bf16[2,64,128]{2,1,0:T(8,128)(2,1)S(1)} async-done(((bf16[2,64,128]{2,1,0:T(8,128)(2,1)}), bf16[2,64,128]{2,1,0:T(8,128)(2,1)S(1)}, u32[]{:S(2)}, u32[]{:S(2)}) %all-to-all-start.3) | async-done | bytes 32800 | tf_op jit(solution)/shard_map/all_to_all | solution.py:31
  129.5 13.8 %all_to_all.54 = f32[64,1,64]{2,1,0:T(1,128)S(1)} all-to-all(f32[64,1,64]{2,1,0:T(1,128)S(1)} %broadcast_in_dim.78), channel_id=1, replica_groups=mesh['kv'=2,'ctx'=64] {'ctx'}, dimensions={0} | all-to-all | bytes 32768 | tf_op jit(solution)/shard_map/all_to_all | solution.py:31
  143.4 0.7 multiply_convert_fusion
  144.1 57.7 %all-gather.2.cloned.1.call-done = bf16[64,8192]{1,0:T(8,128)(2,1)} async-done(((bf16[64,128]{1,0:T(8,128)(2,1)}), bf16[64,8192]{1,0:T(8,128)(2,1)}) %all-gather.2.cloned.1.call-update) | async-done | bytes 1048592 | tf_op jit(solution)/shard_map/all_gather | solution.py:204
  201.8 3.4 %convolution_multiply_fusion.2 = f32[2,32,128]{2,1,0:T(8,128)S(1)} fusion(bf16[2,32,8192]{2,1,0:T(8,128)(2,1)} %bitcast.109, bf16[2,8192,128]{2,1,0:T(8,128)(2,1)} %param.35, f32[2]{0:T(128)S(1)} %get-tuple-element.12), kind=kOutput, calls=%fused_computation.27 | convolution fusion | flops 134225920 | bytes 5275656 | tf_op jit(solution)/shard_map/tqf,tfh->tqh/dot_general | solution.py:212
  205.2 0.6 copy-done.5
  205.8 0.7 convolution_multiply_fusion.3
  208.0 1.0 copy-done.6
  209.0 0.7 convolution_multiply_fusion
  210.2 1.6 copy.156
  211.8 8.6 %all-to-all-start.5 = ((f32[64,128,64]{1,2,0:T(8,128)}), f32[64,128,64]{1,2,0:T(8,128)}, u32[]{:S(2)}, u32[]{:S(2)}) async-start(f32[64,128,64]{1,2,0:T(8,128)} %bitcast.112), calls=%async_computation.5 | async-start | bytes 4194304 | tf_op jit(solution)/shard_map/all_to_all | solution.py:61
  220.4 2.0 sort.35
  222.4 28.1 %all-to-all-done.5 = f32[64,128,64]{1,2,0:T(8,128)} async-done(((f32[64,128,64]{1,2,0:T(8,128)}), f32[64,128,64]{1,2,0:T(8,128)}, u32[]{:S(2)}, u32[]{:S(2)}) %all-to-all-start.5) | async-done | bytes 2097184 | tf_op jit(solution)/shard_map/all_to_all | solution.py:61
  250.5 1.7 reduce_sum.88
  252.3 0.6 broadcast_in_dim.79
  252.9 3.3 %all-to-all-start.6 = ((bf16[2,128,64]{1,2,0:T(8,128)(2,1)}), bf16[2,128,64]{1,2,0:T(8,128)(2,1)S(1)}, u32[]{:S(2)}, u32[]{:S(2)}) async-start(bf16[2,128,64]{1,2,0:T(8,128)(2,1)} %broadcast_in_dim.79), calls=%async_computation.6 | async-start | bytes 65536 | tf_op jit(solution)/shard_map/all_to_all | solution.py:31
  256.2 3.9 %all-to-all-done.6 = bf16[2,128,64]{1,2,0:T(8,128)(2,1)S(1)} async-done(((bf16[2,128,64]{1,2,0:T(8,128)(2,1)}), bf16[2,128,64]{1,2,0:T(8,128)(2,1)S(1)}, u32[]{:S(2)}, u32[]{:S(2)}) %all-to-all-start.6) | async-done | bytes 32800 | tf_op jit(solution)/shard_map/all_to_all | solution.py:31
  260.1 1.2 gather_fusion.7
  (79 shorter events, 7.0 us)
Async XLA Ops:
  6.5 203.2 %copy-start = (bf16[128,8192]{1,0:T(8,128)(2,1)S(1)}, bf16[128,8192]{1,0:T(8,128)(2,1)}, u32[]{:S(2)}) copy-start(bf16[128,8192]{1,0:T(8,128)(2,1)} %param.33) | copy-start | bytes 6291460
  6.5 5.0 %copy-start.2 = (bf16[64,4096]{1,0:T(8,128)(2,1)S(1)}, bf16[64,4096]{1,0:T(8,128)(2,1)}, u32[]{:S(2)}) copy-start(bf16[64,4096]{1,0:T(8,128)(2,1)} %param.20) | copy-start | bytes 1572868
  6.5 6.0 %copy-start.15 = (s32[2]{0:T(128)S(1)}, s32[2]{0:T(128)}, u32[]{:S(2)}) copy-start(s32[2]{0:T(128)} %param.27) | copy-start | bytes 28
  12.4 17.6 %copy-start.9 = (s32[64,64]{1,0:T(8,128)S(1)}, s32[64,64]{1,0:T(8,128)}, u32[]{:S(2)}) copy-start(s32[64,64]{1,0:T(8,128)} %param.26) | copy-start | bytes 49156
  12.6 18.8 %copy-start.7 = (bf16[64,512]{1,0:T(8,128)(2,1)S(1)}, bf16[64,512]{1,0:T(8,128)(2,1)}, u32[]{:S(2)}) copy-start(bf16[64,512]{1,0:T(8,128)(2,1)} %param.21) | copy-start | bytes 196612
  17.5 32.7 %all-to-all-start.1 = ((f32[1,64,32]{2,0,1:T(1,128)}), f32[1,64,32]{2,0,1:T(1,128)S(1)}, u32[]{:S(2)}, u32[]{:S(2)}) async-start(f32[1,64,32]{2,0,1:T(1,128)} %copy.96), calls=%async_computation.1 | async-start | bytes 65536 | tf_op jit(solution)/shard_map/all_to_all | solution.py:160
  33.5 3.5 %copy-start.3 = (f32[2,4,32,8,512]{4,3,2,1,0:T(8,128)S(1)}, f32[2,4,32,8,512]{4,3,2,1,0:T(8,128)}, u32[]{:S(2)}) copy-start(f32[2,4,32,8,512]{4,3,2,1,0:T(8,128)} %get-tuple-element.19) | copy-start | bytes 12582916
  38.3 5.7 %copy-start.8 = (bf16[64,512]{1,0:T(8,128)(2,1)S(1)}, bf16[64,512]{1,0:T(8,128)(2,1)}, u32[]{:S(2)}) copy-start(bf16[64,512]{1,0:T(8,128)(2,1)} %param.22) | copy-start | bytes 196612
  50.2 40.8 %all-to-all-start = ((f32[1,2048,129]{2,0,1:T(1,128)}), f32[1,2048,129]{2,0,1:T(1,128)}, u32[]{:S(2)}, u32[]{:S(2)}) async-start(f32[1,2048,129]{2,0,1:T(1,128)} %copy.94), calls=%async_computation | async-start | bytes 4194304 | tf_op jit(solution)/shard_map/all_to_all | solution.py:18
  62.1 41.7 %copy-start.13 = (f32[2,4]{1,0:T(2,128)S(1)}, f32[2,4]{1,0:T(2,128)}, u32[]{:S(2)}) copy-start(f32[2,4]{1,0:T(2,128)} %param.37) | copy-start | bytes 100
  92.7 1.4 copy-start.4
  94.7 30.7 %copy-start.12 = (bf16[64,128]{1,0:T(8,128)(2,1)S(1)}, bf16[64,128]{1,0:T(8,128)(2,1)}, u32[]{:S(2)}) copy-start(bf16[64,128]{1,0:T(8,128)(2,1)} %param.19) | copy-start | bytes 49156
  95.0 48.4 %copy-start.14 = (f32[128]{0:T(128)S(1)}, f32[128]{0:T(128)}, u32[]{:S(2)}) copy-start(f32[128]{0:T(128)} %param.30) | copy-start | bytes 1540
  98.2 19.5 %all-to-all-start.2 = ((bf16[64,32,128]{2,1,0:T(8,128)(2,1)}), bf16[64,32,128]{2,1,0:T(8,128)(2,1)S(1)}, u32[]{:S(2)}, u32[]{:S(2)}) async-start(bf16[64,32,128]{2,1,0:T(8,128)(2,1)} %broadcast_in_dim.76), calls=%async_computation.2 | async-start | bytes 1048576 | tf_op jit(solution)/shard_map/all_to_all | solution.py:31
  122.2 7.2 %all-to-all-start.3 = ((bf16[2,64,128]{2,1,0:T(8,128)(2,1)}), bf16[2,64,128]{2,1,0:T(8,128)(2,1)S(1)}, u32[]{:S(2)}, u32[]{:S(2)}) async-start(bf16[2,64,128]{2,1,0:T(8,128)(2,1)} %broadcast_in_dim.77), calls=%async_computation.3 | async-start | bytes 65536 | tf_op jit(solution)/shard_map/all_to_all | solution.py:31
  125.4 76.3 %all-gather.2.cloned.1.call-start = ((), (), s32[]{:S(2)}) async-start(), calls=%async_computation.7 | async-start | bytes 1064960 | tf_op jit(solution)/shard_map/all_gather | solution.py:204
  201.8 3.4 %copy-start.1 = (bf16[64,8192]{1,0:T(8,128)(2,1)S(1)}, bf16[64,8192]{1,0:T(8,128)(2,1)}, u32[]{:S(2)}) copy-start(bf16[64,8192]{1,0:T(8,128)(2,1)} %all-gather.2.cloned.1.call-done) | copy-start | bytes 3145732
  201.8 4.1 %copy-start.5 = (bf16[2,8192,128]{2,1,0:T(8,128)(2,1)S(1)}, bf16[2,8192,128]{2,1,0:T(8,128)(2,1)}, u32[]{:S(2)}) copy-start(bf16[2,8192,128]{2,1,0:T(8,128)(2,1)} %param.34) | copy-start | bytes 12582916
  205.2 1.8 copy-start.10
  205.8 1.7 copy-start.11
  206.6 2.4 copy-start.6
  211.8 38.7 %all-to-all-start.5 = ((f32[64,128,64]{1,2,0:T(8,128)}), f32[64,128,64]{1,2,0:T(8,128)}, u32[]{:S(2)}, u32[]{:S(2)}) async-start(f32[64,128,64]{1,2,0:T(8,128)} %bitcast.112), calls=%async_computation.5 | async-start | bytes 4194304 | tf_op jit(solution)/shard_map/all_to_all | solution.py:61
  252.9 7.2 %all-to-all-start.6 = ((bf16[2,128,64]{1,2,0:T(8,128)(2,1)}), bf16[2,128,64]{1,2,0:T(8,128)(2,1)S(1)}, u32[]{:S(2)}, u32[]{:S(2)}) async-start(bf16[2,128,64]{1,2,0:T(8,128)(2,1)} %broadcast_in_dim.79), calls=%async_computation.6 | async-start | bytes 65536 | tf_op jit(solution)/shard_map/all_to_all | solution.py:31
Sparse Core Ops, SparseCore 0:
  144.2 57.4 all-gather.1
where the time goes:
time: 269 us; the launch traced here: 268 us
  waiting for transfers between devices  135 us (50%)
  starting transfers between devices  42.8 us (16%)
  local copies, waits for them, and re-layouts  27.9 us (10%)
  other arithmetic  17.5 us (7%)
  matrix products  16.8 us (6%)
  blocking collectives  13.8 us (5%)
  between operations  13.8 us (5%)
    all_gather x1, waiting for transfers between devices, shards(): piece = lax.all_gather(normed, 'ctx', axis=1, tiled=True)  57.7 us
    all_to_all x1, waiting for transfers between devices, sent_together(): lax.all_to_all(both, axis, split_axis=split_dim, concat_axis=concat_dim,...  28.9 us
    all_to_all x1, waiting for transfers between devices, sum_at_owner(): lax.all_to_all(tiles, axis, split_axis=0, concat_axis=0, tiled=True)  28.1 us
    all_to_all x3, waiting for transfers between devices, sent_to_all(): return lax.all_to_all(copies, axis, split_axis=0, concat_axis=0, tiled=True)  20.9 us
    all_to_all x1, blocking collectives, sent_to_all(): return lax.all_to_all(copies, axis, split_axis=0, concat_axis=0, tiled=True)  13.8 us
    all_to_all x3, starting transfers between devices, sent_to_all(): return lax.all_to_all(copies, axis, split_axis=0, concat_axis=0, tiled=True)  12.1 us
    all_to_all x1, starting transfers between devices, shards(): lax.all_to_all(part_top.reshape(1, all_rows), 'ctx', split_axis=1, concat...  11.5 us
    all_to_all x1, starting transfers between devices, sent_together(): lax.all_to_all(both, axis, split_axis=split_dim, concat_axis=concat_dim,...  10.6 us
  transfers between devices with their start and end apart: 7, of which 6 were waited for; matrix products, arithmetic and copies ran while one was open for 9% of the time, Pallas kernels for 0%

commit v1 on v0

--- a/solution.py
+++ b/solution.py
@@ -9,6 +9,13 @@
 FF = 16384
 NEG = -1e30
 EPS = 1e-05
+
+
+def update_record_for(local_x):
+    formed = jnp.stack([local_x for _ in range(lax.axis_size("ctx"))])
+    aux = lax.all_to_all(formed, axis_name="ctx", split_axis=0, concat_axis=0)
+    y_new = jnp.concatenate(aux, axis=1)
+    return y_new
 
 
 def sent_together(arrays, axis, split_dim, concat_dim, along):
@@ -201,7 +208,7 @@
     squares = of_everyone_2(jnp.sum(hidden * hidden, axis=1), "ctx")
     normed = (hidden * lax.rsqrt(squares / D + EPS)[:, None] * norm_gain).astype(jnp.bfloat16)
     hidden_units = gate_weight.shape[1]
-    piece = lax.all_gather(normed, "ctx", axis=1, tiled=True)
+    piece = update_record_for(normed)
     size = piece.shape[1]
     split_piece = piece.reshape(tenants, draft, size)
     gate_base = jnp.dot(piece, gate_weight, preferred_element_type=jnp.float32)

time: 269 us -> 223 us (0.83)
  waiting for transfers between devices: 135 us -> 77.9 us
  blocking collectives: 13.8 us -> 37.6 us
  between operations: 13.8 us -> 0.46 us
  local copies, waits for them, and re-layouts: 27.9 us -> 32.4 us
  starting transfers between devices: 42.8 us -> 39.8 us
    all_gather x1 -> x0, waiting for transfers between devices: 57.7 us -> none  [shards(): piece = lax.all_gather(normed, 'ctx', axis=1, tiled=True)]
    all_to_all x0 -> x1, blocking collectives: none -> 23.8 us  [update_record_for(): aux = lax.all_to_all(formed, axis_name='ctx', split_axis=0, concat_axis=0)]
    all_to_all x1, starting transfers between devices: 8.58 us -> 5.56 us  [sum_at_owner(): lax.all_to_all(tiles, axis, split_axis=0, concat_axis=0, tiled=True)]
    unnamed x34 -> x36, local copies, waits for them, and re-layouts: 5.29 us -> 6.28 us
  transfers between devices with their start and end apart: 7 -> 6, of which waited for: 6 -> 5; matrix products, arithmetic and copies ran while one was open for 9% -> 11% of each run, Pallas kernels for 0% -> 0%
where the time goes in v1:
time: 223 us; the launch traced here: 222 us
  waiting for transfers between devices  77.9 us (35%)
  starting transfers between devices  39.8 us (18%)
  blocking collectives  37.6 us (17%)
  local copies, waits for them, and re-layouts  32.4 us (15%)
  other arithmetic  16.9 us (8%)
  matrix products  16.6 us (7%)
    all_to_all x1, waiting for transfers between devices, sent_together(): lax.all_to_all(both, axis, split_axis=split_dim, concat_axis=concat_dim,...  28.9 us
    all_to_all x1, waiting for transfers between devices, sum_at_owner(): lax.all_to_all(tiles, axis, split_axis=0, concat_axis=0, tiled=True)  28.1 us
    all_to_all x1, blocking collectives, update_record_for(): aux = lax.all_to_all(formed, axis_name='ctx', split_axis=0, concat_axis=0)  23.8 us
    all_to_all x3, waiting for transfers between devices, sent_to_all(): return lax.all_to_all(copies, axis, split_axis=0, concat_axis=0, tiled=True)  20.9 us
    all_to_all x1, blocking collectives, sent_to_all(): return lax.all_to_all(copies, axis, split_axis=0, concat_axis=0, tiled=True)  13.9 us
    all_to_all x3, starting transfers between devices, sent_to_all(): return lax.all_to_all(copies, axis, split_axis=0, concat_axis=0, tiled=True)  12.1 us
    all_to_all x1, starting transfers between devices, shards(): lax.all_to_all(part_top.reshape(1, all_rows), 'ctx', split_axis=1, concat...  11.5 us
    all_to_all x1, starting transfers between devices, sent_together(): lax.all_to_all(both, axis, split_axis=split_dim, concat_axis=concat_dim,...  10.6 us
  transfers between devices with their start and end apart: 6, of which 5 were waited for; matrix products, arithmetic and copies ran while one was open for 11% of the time, Pallas kernels for 0%

profile of v1, /device:TPU:0, one launch (start us, length us, event | category | flops | bytes accessed | tf_op | source)
XLA Modules:
  0.0 221.5 jit_solution(11853324254874549919)
XLA Ops:
  0.0 2.8 %sort.34 = (s32[64]{0:T(128)}, s32[64]{0:T(128)S(1)}) sort(s32[64]{0:T(128)} %param.25, s32[64]{0:T(128)S(1)} %iota.25), dimensions={0}, to_apply=%region_0.0 | sort | flops 384 | bytes 1024 | tf_op jit(solution)/shard_map/jit(argsort)/sort | solution.py:132
  2.9 2.2 reshape.272
  5.0 0.9 gather_fusion.1
  6.1 4.0 %bitcast_reduce_fusion = (f32[2,32,4,8]{3,1,2,0:T(8,128)S(1)}, f32[2,4,32,8,512]{4,3,2,1,0:T(8,128)}) fusion(pred[2,512]{1,0:T(4,128)(4,1)S(1)} %broadcast_compare_fusion, bf16[2,512,4,128,1]{3,2,1,0,4:T(4,128)(2,1)} %bitcast.126, bf16[2,32,4,8,128]{4,3,2,1,0:T(8,128)(2,1)S(1)} %bitcast.128), kind=kOutput, calls=%fused_computation.12 | convolution fusion | flops 271579136 | bytes 5776384 | tf_op jit(solution)/shard_map/tqgwd,tjgd->tqgwj/dot_general | solution.py:145
  10.3 0.7 copy.101
  11.0 11.5 %all-to-all-start.1 = ((f32[1,64,32]{2,0,1:T(1,128)}), f32[1,64,32]{2,0,1:T(1,128)S(1)}, u32[]{:S(2)}, u32[]{:S(2)}) async-start(f32[1,64,32]{2,0,1:T(1,128)} %copy.101), calls=%async_computation.1 | async-start | bytes 65536 | tf_op jit(solution)/shard_map/all_to_all | solution.py:167
  22.5 1.0 reshape.275
  24.9 0.7 gather_fusion.5
  25.6 1.3 reshape.273
  26.9 3.5 %fusion.4 = f32[2,32,4,8]{3,1,2,0:T(8,128)S(1)} fusion(f32[2,4,32,8,512]{4,3,2,1,0:T(8,128)} %get-tuple-element.19, f32[2,32,4,8]{3,1,2,0:T(8,128)S(1)} %get-tuple-element.18, pred[2,512]{1,0:T(4,128)(4,1)S(1)} %broadcast_compare_fusion), kind=kLoop, calls=%fused_computation.17 | loop fusion | flops 5240832 | bytes 4211712 | tf_op jit(solution)/shard_map/reduce_sum | solution.py:153
  30.5 1.3 fusion.10
  32.0 1.3 reshape_reshape_reshape.8
  33.4 3.2 %pad_maximum_fusion = f32[1,2048,129]{2,1,0:T(8,128)} fusion(f32[1,2048,128]{2,1,0:T(8,128)S(1)} %bitcast.127, f32[1,2048,1]{2,1,0:T(8,128)} %reshape_reshape_reshape.8), kind=kLoop, calls=%fused_computation.19 | loop fusion | flops 264192 | bytes 2113536 | tf_op jit(solution)/shard_map/concatenate | solution.py:23
  36.5 0.8 fusion.13
  37.5 0.7 gather_fusion.6
  38.2 4.8 %copy.99 = f32[1,2048,129]{2,0,1:T(1,128)} copy(f32[1,2048,129]{2,1,0:T(8,128)} %pad_maximum_fusion) | data formatting | bytes 2113536 | tf_op jit(solution)/shard_map/concatenate | solution.py:23
  43.6 10.6 %all-to-all-start = ((f32[1,2048,129]{2,0,1:T(1,128)}), f32[1,2048,129]{2,0,1:T(1,128)}, u32[]{:S(2)}, u32[]{:S(2)}) async-start(f32[1,2048,129]{2,0,1:T(1,128)} %copy.99), calls=%async_computation | async-start | bytes 4194304 | tf_op jit(solution)/shard_map/all_to_all | solution.py:25
  55.6 28.9 %all-to-all-done = f32[1,2048,129]{2,0,1:T(1,128)} async-done(((f32[1,2048,129]{2,0,1:T(1,128)}), f32[1,2048,129]{2,0,1:T(1,128)}, u32[]{:S(2)}, u32[]{:S(2)}) %all-to-all-start) | async-done | bytes 1056800 | tf_op jit(solution)/shard_map/all_to_all | solution.py:25
  84.4 1.7 copy.125
  86.2 1.3 copy-done.5
  87.6 0.6 copy.108
  88.5 2.2 fusion.19
  90.8 0.9 broadcast_in_dim.76
  91.7 5.5 %all-to-all-start.2 = ((bf16[64,32,128]{2,1,0:T(8,128)(2,1)}), bf16[64,32,128]{2,1,0:T(8,128)(2,1)S(1)}, u32[]{:S(2)}, u32[]{:S(2)}) async-start(bf16[64,32,128]{2,1,0:T(8,128)(2,1)} %broadcast_in_dim.76), calls=%async_computation.2 | async-start | bytes 1048576 | tf_op jit(solution)/shard_map/all_to_all | solution.py:38
  97.5 13.7 %all-to-all-done.2 = bf16[64,32,128]{2,1,0:T(8,128)(2,1)S(1)} async-done(((bf16[64,32,128]{2,1,0:T(8,128)(2,1)}), bf16[64,32,128]{2,1,0:T(8,128)(2,1)S(1)}, u32[]{:S(2)}, u32[]{:S(2)}) %all-to-all-start.2) | async-done | bytes 524320 | tf_op jit(solution)/shard_map/all_to_all | solution.py:38
  111.4 2.0 convolution_multiply_fusion.4
  113.4 1.6 fusion.16
  115.6 3.3 %all-to-all-start.3 = ((bf16[2,64,128]{2,1,0:T(8,128)(2,1)}), bf16[2,64,128]{2,1,0:T(8,128)(2,1)S(1)}, u32[]{:S(2)}, u32[]{:S(2)}) async-start(bf16[2,64,128]{2,1,0:T(8,128)(2,1)} %broadcast_in_dim.77), calls=%async_computation.3 | async-start | bytes 65536 | tf_op jit(solution)/shard_map/all_to_all | solution.py:38
  118.9 0.6 gather_fusion
  119.6 3.3 %all-to-all-done.3 = bf16[2,64,128]{2,1,0:T(8,128)(2,1)S(1)} async-done(((bf16[2,64,128]{2,1,0:T(8,128)(2,1)}), bf16[2,64,128]{2,1,0:T(8,128)(2,1)S(1)}, u32[]{:S(2)}, u32[]{:S(2)}) %all-to-all-start.3) | async-done | bytes 32800 | tf_op jit(solution)/shard_map/all_to_all | solution.py:38
  123.0 13.9 %all_to_all.59 = f32[64,1,64]{2,1,0:T(1,128)S(1)} all-to-all(f32[64,1,64]{2,1,0:T(1,128)S(1)} %broadcast_in_dim.78), channel_id=1, replica_groups=mesh['kv'=2,'ctx'=64] {'ctx'}, dimensions={0} | all-to-all | bytes 32768 | tf_op jit(solution)/shard_map/all_to_all | solution.py:38
  137.2 23.8 %all_to_all.60 = bf16[64,64,128]{2,1,0:T(8,128)(2,1)S(1)} all-to-all(bf16[64,64,128]{2,1,0:T(8,128)(2,1)S(1)} %stack.2), channel_id=1, replica_groups=mesh['kv'=2,'ctx'=64] {'ctx'}, dimensions={0} | all-to-all | bytes 2097152 | tf_op jit(solution)/shard_map/all_to_all | solution.py:16
  161.0 1.0 copy-done.3
  162.0 1.7 copy.110
  163.7 1.5 reshape_reshape.12
  165.2 3.1 %convolution_multiply_fusion.2 = f32[2,32,128]{2,1,0:T(8,128)S(1)} fusion(bf16[2,32,8192]{2,1,0:T(8,128)(2,1)S(1)} %reshape_reshape.12, bf16[2,8192,128]{2,1,0:T(8,128)(2,1)} %param.35, f32[2]{0:T(128)S(1)} %get-tuple-element.12), kind=kOutput, calls=%fused_computation.27 | convolution fusion | flops 134225920 | bytes 5275656 | tf_op jit(solution)/shard_map/tqf,tfh->tqh/dot_general | solution.py:219
  168.6 0.8 convolution_multiply_fusion.3
  169.6 0.7 copy-done.11
  171.4 0.8 copy-done.7
  172.3 0.7 convolution_multiply_fusion
  173.5 1.6 copy.172
  175.0 5.6 %all-to-all-start.6 = ((f32[64,128,64]{1,2,0:T(8,128)}), f32[64,128,64]{1,2,0:T(8,128)}, u32[]{:S(2)}, u32[]{:S(2)}) async-start(f32[64,128,64]{1,2,0:T(8,128)} %bitcast.121), calls=%async_computation.6 | async-start | bytes 4194304 | tf_op jit(solution)/shard_map/all_to_all | solution.py:68
  180.6 2.0 sort.35
  182.7 28.1 %all-to-all-done.6 = f32[64,128,64]{1,2,0:T(8,128)} async-done(((f32[64,128,64]{1,2,0:T(8,128)}), f32[64,128,64]{1,2,0:T(8,128)}, u32[]{:S(2)}, u32[]{:S(2)}) %all-to-all-start.6) | async-done | bytes 2097184 | tf_op jit(solution)/shard_map/all_to_all | solution.py:68
  210.8 1.7 reduce_sum.88
  213.1 3.3 %all-to-all-start.7 = ((bf16[2,128,64]{1,2,0:T(8,128)(2,1)}), bf16[2,128,64]{1,2,0:T(8,128)(2,1)S(1)}, u32[]{:S(2)}, u32[]{:S(2)}) async-start(bf16[2,128,64]{1,2,0:T(8,128)(2,1)} %broadcast_in_dim.79), calls=%async_computation.7 | async-start | bytes 65536 | tf_op jit(solution)/shard_map/all_to_all | solution.py:38
  216.4 3.9 %all-to-all-done.7 = bf16[2,128,64]{1,2,0:T(8,128)(2,1)S(1)} async-done(((bf16[2,128,64]{1,2,0:T(8,128)(2,1)}), bf16[2,128,64]{1,2,0:T(8,128)(2,1)S(1)}, u32[]{:S(2)}, u32[]{:S(2)}) %all-to-all-start.7) | async-done | bytes 32800 | tf_op jit(solution)/shard_map/all_to_all | solution.py:38
  220.3 1.2 gather_fusion.7
  (82 shorter events, 8.7 us)
Async XLA Ops:
  0.0 172.9 %copy-start = (bf16[128,8192]{1,0:T(8,128)(2,1)S(1)}, bf16[128,8192]{1,0:T(8,128)(2,1)}, u32[]{:S(2)}) copy-start(bf16[128,8192]{1,0:T(8,128)(2,1)} %param.33) | copy-start | bytes 6291460
  0.0 5.0 %copy-start.1 = (bf16[64,4096]{1,0:T(8,128)(2,1)S(1)}, bf16[64,4096]{1,0:T(8,128)(2,1)}, u32[]{:S(2)}) copy-start(bf16[64,4096]{1,0:T(8,128)(2,1)} %param.20) | copy-start | bytes 1572868
  0.0 6.0 %copy-start.16 = (s32[2]{0:T(128)S(1)}, s32[2]{0:T(128)}, u32[]{:S(2)}) copy-start(s32[2]{0:T(128)} %param.27) | copy-start | bytes 28
  5.9 17.6 %copy-start.10 = (s32[64,64]{1,0:T(8,128)S(1)}, s32[64,64]{1,0:T(8,128)}, u32[]{:S(2)}) copy-start(s32[64,64]{1,0:T(8,128)} %param.26) | copy-start | bytes 49156
  6.0 18.8 %copy-start.8 = (bf16[64,512]{1,0:T(8,128)(2,1)S(1)}, bf16[64,512]{1,0:T(8,128)(2,1)}, u32[]{:S(2)}) copy-start(bf16[64,512]{1,0:T(8,128)(2,1)} %param.21) | copy-start | bytes 196612
  11.0 32.7 %all-to-all-start.1 = ((f32[1,64,32]{2,0,1:T(1,128)}), f32[1,64,32]{2,0,1:T(1,128)S(1)}, u32[]{:S(2)}, u32[]{:S(2)}) async-start(f32[1,64,32]{2,0,1:T(1,128)} %copy.101), calls=%async_computation.1 | async-start | bytes 65536 | tf_op jit(solution)/shard_map/all_to_all | solution.py:167
  26.9 3.5 %copy-start.2 = (f32[2,4,32,8,512]{4,3,2,1,0:T(8,128)S(1)}, f32[2,4,32,8,512]{4,3,2,1,0:T(8,128)}, u32[]{:S(2)}) copy-start(f32[2,4,32,8,512]{4,3,2,1,0:T(8,128)} %get-tuple-element.19) | copy-start | bytes 12582916
  31.8 5.7 %copy-start.9 = (bf16[64,512]{1,0:T(8,128)(2,1)S(1)}, bf16[64,512]{1,0:T(8,128)(2,1)}, u32[]{:S(2)}) copy-start(bf16[64,512]{1,0:T(8,128)(2,1)} %param.22) | copy-start | bytes 196612
  43.6 40.8 %all-to-all-start = ((f32[1,2048,129]{2,0,1:T(1,128)}), f32[1,2048,129]{2,0,1:T(1,128)}, u32[]{:S(2)}, u32[]{:S(2)}) async-start(f32[1,2048,129]{2,0,1:T(1,128)} %copy.99), calls=%async_computation | async-start | bytes 4194304 | tf_op jit(solution)/shard_map/all_to_all | solution.py:25
  55.5 41.7 %copy-start.14 = (f32[2,4]{1,0:T(2,128)S(1)}, f32[2,4]{1,0:T(2,128)}, u32[]{:S(2)}) copy-start(f32[2,4]{1,0:T(2,128)} %param.37) | copy-start | bytes 100
  86.1 1.4 copy-start.5
  88.2 30.7 %copy-start.13 = (bf16[64,128]{1,0:T(8,128)(2,1)S(1)}, bf16[64,128]{1,0:T(8,128)(2,1)}, u32[]{:S(2)}) copy-start(bf16[64,128]{1,0:T(8,128)(2,1)} %param.19) | copy-start | bytes 49156
  88.5 48.4 %copy-start.15 = (f32[128]{0:T(128)S(1)}, f32[128]{0:T(128)}, u32[]{:S(2)}) copy-start(f32[128]{0:T(128)} %param.30) | copy-start | bytes 1540
  91.7 19.5 %all-to-all-start.2 = ((bf16[64,32,128]{2,1,0:T(8,128)(2,1)}), bf16[64,32,128]{2,1,0:T(8,128)(2,1)S(1)}, u32[]{:S(2)}, u32[]{:S(2)}) async-start(bf16[64,32,128]{2,1,0:T(8,128)(2,1)} %broadcast_in_dim.76), calls=%async_computation.2 | async-start | bytes 1048576 | tf_op jit(solution)/shard_map/all_to_all | solution.py:38
  115.6 7.2 %all-to-all-start.3 = ((bf16[2,64,128]{2,1,0:T(8,128)(2,1)}), bf16[2,64,128]{2,1,0:T(8,128)(2,1)S(1)}, u32[]{:S(2)}, u32[]{:S(2)}) async-start(bf16[2,64,128]{2,1,0:T(8,128)(2,1)} %broadcast_in_dim.77), calls=%async_computation.3 | async-start | bytes 65536 | tf_op jit(solution)/shard_map/all_to_all | solution.py:38
  161.0 1.0 copy-start.3
  165.2 3.5 %copy-start.6 = (bf16[2,8192,128]{2,1,0:T(8,128)(2,1)S(1)}, bf16[2,8192,128]{2,1,0:T(8,128)(2,1)}, u32[]{:S(2)}) copy-start(bf16[2,8192,128]{2,1,0:T(8,128)(2,1)} %param.34) | copy-start | bytes 12582916
  168.3 1.3 copy-start.4
  168.3 2.0 copy-start.11
  168.6 2.2 %copy-start.12 = (bf16[8192,128]{1,0:T(8,128)(2,1)S(1)}, bf16[8192,128]{1,0:T(8,128)(2,1)}, u32[]{:S(2)}) copy-start(bf16[8192,128]{1,0:T(8,128)(2,1)} %param.32) | copy-start | bytes 6291460
  169.4 2.8 %copy-start.7 = (bf16[2,128,8192]{2,1,0:T(8,128)(2,1)S(1)}, bf16[2,128,8192]{2,1,0:T(8,128)(2,1)}, u32[]{:S(2)}) copy-start(bf16[2,128,8192]{2,1,0:T(8,128)(2,1)} %param.36) | copy-start | bytes 12582916
  175.0 35.7 %all-to-all-start.6 = ((f32[64,128,64]{1,2,0:T(8,128)}), f32[64,128,64]{1,2,0:T(8,128)}, u32[]{:S(2)}, u32[]{:S(2)}) async-start(f32[64,128,64]{1,2,0:T(8,128)} %bitcast.121), calls=%async_computation.6 | async-start | bytes 4194304 | tf_op jit(solution)/shard_map/all_to_all | solution.py:68
  213.1 7.2 %all-to-all-start.7 = ((bf16[2,128,64]{1,2,0:T(8,128)(2,1)}), bf16[2,128,64]{1,2,0:T(8,128)(2,1)S(1)}, u32[]{:S(2)}, u32[]{:S(2)}) async-start(bf16[2,128,64]{1,2,0:T(8,128)(2,1)} %broadcast_in_dim.79), calls=%async_computation.7 | async-start | bytes 65536 | tf_op jit(solution)/shard_map/all_to_all | solution.py:38
